TPU v7x, 32 devices: a whole 2x2x4 slice. The times are simulated.
32 devices in a mesh: slab: 8 (over z, y), patch: 4 (over x, core).
Axes of the slice: x: 2, y: 2, z: 4, core: 2. Of those that a mesh axis runs over, the one named last changes fastest.
Arguments:
- fluid_state: float32 [16, 256, 256], P('slab', 'patch'), may hold values from -6 to 6
- fluid_rhs: float32 [16, 256, 256], P('slab', 'patch'), may hold values from -24 to 24
- element_scale: float32 [16, 256], P('slab', 'patch'), may hold values from 1 to 4
- element_matrix: bfloat16 [256, 256], replicated
- couple_x: bfloat16 [256, 256], replicated, may hold values from -0.09375 to 0.09375
- couple_y: bfloat16 [256, 256], replicated, may hold values from -0.09375 to 0.09375
- block_inverse: bfloat16 [256, 256], replicated
- traction_map: bfloat16 [3, 256], replicated, may hold values from -0.375 to 0.375
- slot_elem: int32 [8, 4, 1024], P('slab', 'patch'), may hold values from 0 to 127
- slot_point: int32 [8, 4, 1024], P('slab', 'patch'), may hold values from 0 to 8191
- slot_count: int32 [8, 4, 4], P('slab', 'patch'), may hold values from 0 to 256, as said below
- displacement: float32 [3, 256, 128], P(None, 'patch'), may hold values from -6 to 6
- stiffness: float32 [256, 128], P('patch'), may hold values from 0.03 to 0.3
Outputs:
- fluid_out: float32 [16, 256, 256], P('slab', 'patch')
- displacement_new: float32 [3, 256, 128], P(None, 'patch')
- wall_motion: float32 [3, 8, 4, 1024], P(None, 'slab', 'patch')
Inputs may be any that keep to these rules, and one draw needn't show every extreme that they name: For every block and owner only the first slot_count slots of that owner's 256 slots are live; the count 256 is reached for some block and owner in every draw.
All inputs are finite; a program needn't handle non-finite values.
Results may differ from a plain program's by a relative error of at most 0.0049.
Values may be sent and summed in bfloat16 or wider, within the bound.
A program may use at most 128 MiB of HBM per device.

v0:
```python
import jax
import jax.numpy as jnp
from jax import lax
from jax.sharding import PartitionSpec as P

SWEEPS = 3


def with_halo(cells, sides, width):
    for axis, dim in sides:
        count = lax.axis_size(axis)
        ends = count - 1
        head = lax.slice_in_dim(cells, 0, width, axis=dim)
        tail = lax.slice_in_dim(cells, cells.shape[dim] - width, cells.shape[dim], axis=dim)
        cells = jnp.concatenate(
            [
                lax.ppermute(tail, axis, [(i, (i + 1) % count) for i in range(ends)]),
                cells,
                lax.ppermute(head, axis, [((i + 1) % count, i) for i in range(ends)]),
            ],
            axis=dim,
        )
    return cells


def element_apply(rounded, scale, element_matrix, couple_x, couple_y):
    padded = with_halo(rounded, (("slab", 0), ("patch", 1)), 1)
    along_x = (padded[:-2, 1:-1].astype(jnp.float32) + padded[2:, 1:-1].astype(jnp.float32)).astype(
        jnp.bfloat16
    )
    along_y = (padded[1:-1, :-2].astype(jnp.float32) + padded[1:-1, 2:].astype(jnp.float32)).astype(
        jnp.bfloat16
    )
    width = rounded.shape[2]
    own = jnp.dot(rounded.reshape(-1, width), element_matrix, preferred_element_type=jnp.float32)
    side_x = jnp.dot(along_x.reshape(-1, width), couple_x, preferred_element_type=jnp.float32)
    side_y = jnp.dot(along_y.reshape(-1, width), couple_y, preferred_element_type=jnp.float32)
    return (
        scale[:, :, None] * own.reshape(rounded.shape)
        - side_x.reshape(rounded.shape)
        - side_y.reshape(rounded.shape)
    )


def laplace_net(field):
    edged = with_halo(field.astype(jnp.bfloat16), (("patch", 1),), 1).astype(field.dtype)
    edged = jnp.pad(edged, ((0, 0), (0, 0), (1, 1)))
    return 4.0 * field - (
        edged[:, 2:, 1:-1] + edged[:, :-2, 1:-1] + edged[:, 1:-1, 2:] + edged[:, 1:-1, :-2]
    )


def shards(
    fluid_state,
    fluid_rhs,
    element_scale,
    element_matrix,
    couple_x,
    couple_y,
    block_inverse,
    traction_map,
    slot_elem,
    slot_point,
    slot_count,
    displacement,
    stiffness,
):
    width = fluid_state.shape[2]
    state = fluid_state
    for sweep in range(SWEEPS):
        rounded = state.astype(jnp.bfloat16)
        applied = element_apply(rounded, element_scale, element_matrix, couple_x, couple_y)
        residue = (fluid_rhs - applied).astype(jnp.bfloat16)
        update = jnp.dot(
            residue.reshape(-1, width), block_inverse, preferred_element_type=jnp.float32
        ).reshape(state.shape)
        state = state + update / element_scale[:, :, None]
    final = state.astype(jnp.bfloat16)
    owners = lax.axis_size("patch")
    capacity = slot_elem.shape[2] // owners
    net_rows = displacement.shape[1]
    net_cols = displacement.shape[2]
    cells = net_rows * net_cols
    rows = jnp.take(final.reshape(-1, width), slot_elem.reshape(-1), axis=0).reshape(
        owners, capacity, width
    )
    pull = jnp.einsum("cd,kqd->kcq", traction_map, rows, preferred_element_type=jnp.float32)
    limits = slot_count.reshape(owners)
    live = (lax.broadcasted_iota(jnp.int32, (owners, capacity), 1) < limits[:, None]).astype(
        jnp.float32
    )
    pull = pull * live[:, None, :]
    points = slot_point.reshape(owners, capacity)
    owner_ids = lax.broadcasted_iota(jnp.int32, (owners, capacity), 0)
    got_pull, got_points = (
        lax.all_to_all(pull, "patch", split_axis=0, concat_axis=0, tiled=True),
        lax.all_to_all(points, "patch", split_axis=0, concat_axis=0, tiled=True),
    )
    local = jnp.zeros((3, cells), jnp.float32)
    local = local.at[:, got_points.reshape(-1)].add(got_pull.transpose(1, 0, 2).reshape(3, -1))
    loads = lax.psum(local, "slab")
    loads = loads.reshape(3, net_rows, net_cols)
    bend = laplace_net(displacement)
    stiff_term = stiffness[None] * (laplace_net(bend) + 4.0 * bend)
    displacement_new = displacement + (loads - stiff_term) / (36.0 * stiffness[None])
    flat_net = displacement_new.reshape(3, -1)
    whole = lax.all_gather(flat_net, "patch", axis=1, tiled=True)
    picked = whole[:, (owner_ids * cells + points).reshape(-1)]
    wall_motion = (picked * live.reshape(1, -1)).reshape(3, 1, 1, owners * capacity)
    return (state, displacement_new, wall_motion)


def solution(mesh):
    return jax.shard_map(
        shards,
        mesh=mesh,
        in_specs=(
            P("slab", "patch", None),
            P("slab", "patch", None),
            P("slab", "patch"),
            P(),
            P(),
            P(),
            P(),
            P(),
            P("slab", "patch", None),
            P("slab", "patch", None),
            P("slab", "patch", None),
            P(None, "patch", None),
            P("patch", None),
        ),
        out_specs=(
            P("slab", "patch", None),
            P(None, "patch", None),
            P(None, "slab", "patch", None),
        ),
        check_vma=False,
    )
```

profile of v0, /device:TPU:0, one launch (start us, length us, event | category | flops | bytes accessed | tf_op | source)
XLA Modules:
  0.0 299.1 jit_solution(18253544204650045127)
XLA Ops:
  7.2 1.0 convert_element_type.106
  8.3 1.3 collective-permute-start.1
  9.6 5.5 %collective-permute-start = (bf16[1,64,256]{2,1,0:T(8,128)(2,1)S(1)}, bf16[1,64,256]{2,1,0:T(8,128)(2,1)S(1)}, u32[]{:S(2)}, u32[]{:S(2)}) collective-permute-start(bf16[1,64,256]{2,1,0:T(8,128)(2,1)S(1)} %get-tuple-element.24), channel_id=1, source_target_pairs={{0,4},{4,8},{8,12},{12,16},{16,20},{20,24},{24,28},{1,5},{5,9},{9,... | collective-permute-start | bytes 98312 | tf_op jit(solution)/shard_map/ppermute | solution.py:17
  15.1 3.3 %all-to-all-start = ((s32[4,1,256]{2,1,0:T(1,128)}), s32[4,1,256]{2,1,0:T(1,128)S(1)}, u32[]{:S(2)}, u32[]{:S(2)}) async-start(s32[4,1,256]{2,1,0:T(1,128)} %bitcast.90), calls=%async_computation | async-start | bytes 8192 | tf_op jit(solution)/shard_map/all_to_all | solution.py:97
  18.4 0.9 convert_element_type.132
  19.3 1.3 collective-permute-start.13
  20.6 3.0 %collective-permute-start.12 = (bf16[3,1,128]{2,1,0:T(2,128)(2,1)S(1)}, bf16[3,1,128]{2,1,0:T(2,128)(2,1)S(1)}, u32[]{:S(2)}, u32[]{:S(2)}) collective-permute-start(bf16[3,1,128]{2,1,0:T(2,128)(2,1)S(1)} %get-tuple-element.28), channel_id=1, source_target_pairs={{0,1},{1,2},{2,3},{4,5},{5,6},{6,7},{8,9},{9,10},{10,11},{12,13},{... | collective-permute-start | bytes 2312 | tf_op jit(solution)/shard_map/ppermute | solution.py:17
  23.7 0.7 compare_select_fusion.1
  24.4 0.5 broadcast.126
  24.9 1.3 reduce.3
  26.2 0.8 broadcast_multiply_fusion
  27.1 0.7 compare_select_fusion
  27.8 1.1 convolution_multiply_fusion.2
  28.8 0.7 fusion.59
  29.6 1.0 fusion.70
  30.7 1.3 collective-permute-start.15
  32.0 4.3 %collective-permute-start.14 = (bf16[3,1,128]{2,1,0:T(2,128)(2,1)S(1)}, bf16[3,1,128]{2,1,0:T(2,128)(2,1)S(1)}, u32[]{:S(2)}, u32[]{:S(2)}) collective-permute-start(bf16[3,1,128]{2,1,0:T(2,128)(2,1)S(1)} %get-tuple-element.26), channel_id=1, source_target_pairs={{0,1},{1,2},{2,3},{4,5},{5,6},{6,7},{8,9},{9,10},{10,11},{12,13},{... | collective-permute-start | bytes 2312 | tf_op jit(solution)/shard_map/ppermute | solution.py:17
  36.3 1.3 collective-permute-start.3
  37.6 4.3 %collective-permute-start.2 = (bf16[4,1,256]{2,1,0:T(2,128)(2,1)S(1)}, bf16[4,1,256]{2,1,0:T(2,128)(2,1)S(1)}, u32[]{:S(2)}, u32[]{:S(2)}) collective-permute-start(bf16[4,1,256]{2,1,0:T(2,128)(2,1)S(1)} %get-tuple-element.18), channel_id=1, source_target_pairs={{0,1},{1,2},{2,3},{4,5},{5,6},{6,7},{8,9},{9,10},{10,11},{12,13},{... | collective-permute-start | bytes 6152 | tf_op jit(solution)/shard_map/ppermute | solution.py:17
  41.9 1.1 convolution_subtract_fusion.5
  43.0 1.3 fusion.77
  44.3 1.3 collective-permute-start.5
  45.6 5.4 %collective-permute-start.4 = (bf16[1,64,256]{2,1,0:T(8,128)(2,1)S(1)}, bf16[1,64,256]{2,1,0:T(8,128)(2,1)S(1)}, u32[]{:S(2)}, u32[]{:S(2)}) collective-permute-start(bf16[1,64,256]{2,1,0:T(8,128)(2,1)S(1)} %get-tuple-element.22), channel_id=1, source_target_pairs={{0,4},{4,8},{8,12},{12,16},{16,20},{20,24},{24,28},{1,5},{5,9},{9,... | collective-permute-start | bytes 98312 | tf_op jit(solution)/shard_map/ppermute | solution.py:17
  51.1 1.1 convolution_multiply_fusion.1
  52.1 0.5 collective-permute-done.4
  52.6 1.3 collective-permute-start.7
  53.9 3.5 %collective-permute-start.6 = (bf16[4,1,256]{2,1,0:T(2,128)(2,1)S(1)}, bf16[4,1,256]{2,1,0:T(2,128)(2,1)S(1)}, u32[]{:S(2)}, u32[]{:S(2)}) collective-permute-start(bf16[4,1,256]{2,1,0:T(2,128)(2,1)S(1)} %get-tuple-element.16), channel_id=1, source_target_pairs={{0,1},{1,2},{2,3},{4,5},{5,6},{6,7},{8,9},{9,10},{10,11},{12,13},{... | collective-permute-start | bytes 6152 | tf_op jit(solution)/shard_map/ppermute | solution.py:17
  57.7 0.6 collective-permute-done.6
  58.3 0.3 fusion.80
  58.6 1.3 collective-permute-start.9
  59.9 5.2 %collective-permute-start.8 = (bf16[1,64,256]{2,1,0:T(8,128)(2,1)S(1)}, bf16[1,64,256]{2,1,0:T(8,128)(2,1)S(1)}, u32[]{:S(2)}, u32[]{:S(2)}) collective-permute-start(bf16[1,64,256]{2,1,0:T(8,128)(2,1)S(1)} %get-tuple-element.20), channel_id=1, source_target_pairs={{0,4},{4,8},{8,12},{12,16},{16,20},{20,24},{24,28},{1,5},{5,9},{9,... | collective-permute-start | bytes 98312 | tf_op jit(solution)/shard_map/ppermute | solution.py:17
  65.3 1.4 collective-permute-done.8
  66.7 1.3 collective-permute-start.11
  68.0 4.5 %collective-permute-start.10 = (bf16[4,1,256]{2,1,0:T(2,128)(2,1)S(1)}, bf16[4,1,256]{2,1,0:T(2,128)(2,1)S(1)}, u32[]{:S(2)}, u32[]{:S(2)}) collective-permute-start(bf16[4,1,256]{2,1,0:T(2,128)(2,1)S(1)} %get-tuple-element.14), channel_id=1, source_target_pairs={{0,1},{1,2},{2,3},{4,5},{5,6},{6,7},{8,9},{9,10},{10,11},{12,13},{... | collective-permute-start | bytes 6152 | tf_op jit(solution)/shard_map/ppermute | solution.py:17
  72.7 0.6 collective-permute-done.10
  73.3 1.0 fusion.83
  74.3 3.9 %gather_fusion = bf16[1024,256]{1,0:T(8,128)(2,1)S(1)} fusion(bf16[128,256]{1,0:T(8,128)(2,1)S(1)} %bitcast.84, s32[1024]{0:T(1024)S(1)} %broadcast_clamp_fusion.1), kind=kCustom, calls=%fused_computation | custom fusion | bytes 1052672 | tf_op jit(solution)/shard_map/jit(_take)/gather | solution.py:84
  78.3 0.9 fusion.11
  79.2 6.5 %all-to-all-start.1 = ((f32[4,3,256]{2,1,0:T(4,128)}), f32[4,3,256]{2,1,0:T(4,128)S(1)}, u32[]{:S(2)}, u32[]{:S(2)}) async-start(f32[4,3,256]{2,1,0:T(4,128)} %fusion.11), calls=%async_computation.1 | async-start | bytes 32768 | tf_op jit(solution)/shard_map/all_to_all | solution.py:96
  85.7 3.8 %all-to-all-done.1 = f32[4,3,256]{2,1,0:T(4,128)S(1)} async-done(((f32[4,3,256]{2,1,0:T(4,128)}), f32[4,3,256]{2,1,0:T(4,128)S(1)}, u32[]{:S(2)}, u32[]{:S(2)}) %all-to-all-start.1) | async-done | bytes 12320 | tf_op jit(solution)/shard_map/all_to_all | solution.py:96
  89.8 8.2 %scatter_custom_fusion = f32[3,8192]{0,1:T(8,128)} fusion(s32[1024]{0:T(1024)S(1)} %bitcast.95, f32[1024,3]{1,0:T(8,128)S(1)} %copy.23, f32[]{:T(128)} %constant.9.clone.1), kind=kCustom, calls=%fused_computation.3 | custom fusion | flops 3072 | bytes 98308 | tf_op jit(solution)/shard_map/scatter-add | solution.py:100
  98.0 3.5 %copy.24 = f32[3,64,128]{2,1,0:T(8,128)} copy(f32[3,64,128]{0,2,1:T(8,128)} %bitcast.86) | data formatting | bytes 196608 | tf_op jit(solution)/shard_map/reshape | solution.py:102
  101.6 73.6 %all-reduce.4.cloned.1.call-done = f32[3,64,128]{2,1,0:T(8,128)} async-done(((f32[3,64,128]{2,1,0:T(8,128)}), f32[3,64,128]{2,1,0:T(8,128)}) %all-reduce.4.cloned.1.call-update) | async-done | bytes 98320 | tf_op jit(solution)/shard_map/psum | solution.py:101
  175.2 1.0 fusion.33
  176.2 2.6 copy.25
  178.8 103.9 %all_gather.3 = f32[3,32768]{0,1:T(8,128)} all-gather(f32[3,8192]{0,1:T(8,128)} %bitcast.85), channel_id=1, replica_groups=mesh['slab'=8,'patch'=4] {'patch'}, dimensions={1}, use_global_device_ids=true | all-gather | bytes 491520 | tf_op jit(solution)/shard_map/all_gather | solution.py:107
  282.7 8.6 %gather_fusion.1 = f32[1024,3]{1,0:T(8,128)S(1)} fusion(f32[3,32768]{0,1:T(8,128)} %all_gather.3, s32[1024]{0:T(1024)S(1)} %broadcast_clamp_fusion), kind=kCustom, calls=%fused_computation.1 | custom fusion | bytes 28672 | tf_op jit(solution)/shard_map/gather | solution.py:108
  291.5 0.8 copy.26
  (58 shorter events, 1.3 us)
Async XLA Ops:
  7.2 35.8 %copy-start = (bf16[256,256]{1,0:T(8,128)(2,1)S(1)}, bf16[256,256]{1,0:T(8,128)(2,1)}, u32[]{:S(2)}) copy-start(bf16[256,256]{1,0:T(8,128)(2,1)} %param.19) | copy-start | bytes 393220
  7.2 51.1 %copy-start.6 = (f32[2,64]{1,0:T(2,128)S(1)}, f32[2,64]{1,0:T(2,128)}, u32[]{:S(2)}) copy-start(f32[2,64]{1,0:T(2,128)} %param.15) | copy-start | bytes 1540
  7.2 57.9 %copy-start.1 = (bf16[256,256]{1,0:T(8,128)(2,1)S(1)}, bf16[256,256]{1,0:T(8,128)(2,1)}, u32[]{:S(2)}) copy-start(bf16[256,256]{1,0:T(8,128)(2,1)} %param.16) | copy-start | bytes 393220
  7.2 50.3 %copy-start.2 = (bf16[256,256]{1,0:T(8,128)(2,1)S(1)}, bf16[256,256]{1,0:T(8,128)(2,1)}, u32[]{:S(2)}) copy-start(bf16[256,256]{1,0:T(8,128)(2,1)} %param.17) | copy-start | bytes 393220
  7.2 51.1 %copy-start.7 = (f32[2,64,256]{2,1,0:T(8,128)S(1)}, f32[2,64,256]{2,1,0:T(8,128)}, u32[]{:S(2)}) copy-start(f32[2,64,256]{2,1,0:T(8,128)} %param.14) | copy-start | bytes 393220
  7.2 51.1 %copy-start.8 = (bf16[256,256]{1,0:T(8,128)(2,1)S(1)}, bf16[256,256]{1,0:T(8,128)(2,1)}, u32[]{:S(2)}) copy-start(bf16[256,256]{1,0:T(8,128)(2,1)} %param.18) | copy-start | bytes 393220
  8.3 28.0 %collective-permute-start.1 = (bf16[1,64,256]{2,1,0:T(8,128)(2,1)S(1)}, bf16[1,64,256]{2,1,0:T(8,128)(2,1)S(1)}, u32[]{:S(2)}, u32[]{:S(2)}) collective-permute-start(bf16[1,64,256]{2,1,0:T(8,128)(2,1)S(1)} %get-tuple-element.25), channel_id=1, source_target_pairs={{4,0},{8,4},{12,8},{16,12},{20,16},{24,20},{28,24},{5,1},{9,5},{13... | collective-permute-start | bytes 98312 | tf_op jit(solution)/shard_map/ppermute | solution.py:19
  9.6 26.7 %collective-permute-start = (bf16[1,64,256]{2,1,0:T(8,128)(2,1)S(1)}, bf16[1,64,256]{2,1,0:T(8,128)(2,1)S(1)}, u32[]{:S(2)}, u32[]{:S(2)}) collective-permute-start(bf16[1,64,256]{2,1,0:T(8,128)(2,1)S(1)} %get-tuple-element.24), channel_id=1, source_target_pairs={{0,4},{4,8},{8,12},{12,16},{16,20},{20,24},{24,28},{1,5},{5,9},{9,... | collective-permute-start | bytes 98312 | tf_op jit(solution)/shard_map/ppermute | solution.py:17
  15.1 64.1 %all-to-all-start = ((s32[4,1,256]{2,1,0:T(1,128)}), s32[4,1,256]{2,1,0:T(1,128)S(1)}, u32[]{:S(2)}, u32[]{:S(2)}) async-start(s32[4,1,256]{2,1,0:T(1,128)} %bitcast.90), calls=%async_computation | async-start | bytes 8192 | tf_op jit(solution)/shard_map/all_to_all | solution.py:97
  19.3 10.3 %collective-permute-start.13 = (bf16[3,1,128]{2,1,0:T(2,128)(2,1)S(1)}, bf16[3,1,128]{2,1,0:T(2,128)(2,1)S(1)}, u32[]{:S(2)}, u32[]{:S(2)}) collective-permute-start(bf16[3,1,128]{2,1,0:T(2,128)(2,1)S(1)} %get-tuple-element.29), channel_id=1, source_target_pairs={{1,0},{2,1},{3,2},{5,4},{6,5},{7,6},{9,8},{10,9},{11,10},{13,12},{... | collective-permute-start | bytes 2312 | tf_op jit(solution)/shard_map/ppermute | solution.py:19
  20.6 9.0 %collective-permute-start.12 = (bf16[3,1,128]{2,1,0:T(2,128)(2,1)S(1)}, bf16[3,1,128]{2,1,0:T(2,128)(2,1)S(1)}, u32[]{:S(2)}, u32[]{:S(2)}) collective-permute-start(bf16[3,1,128]{2,1,0:T(2,128)(2,1)S(1)} %get-tuple-element.28), channel_id=1, source_target_pairs={{0,1},{1,2},{2,3},{4,5},{5,6},{6,7},{8,9},{9,10},{10,11},{12,13},{... | collective-permute-start | bytes 2312 | tf_op jit(solution)/shard_map/ppermute | solution.py:17
  30.7 70.8 %collective-permute-start.15 = (bf16[3,1,128]{2,1,0:T(2,128)(2,1)S(1)}, bf16[3,1,128]{2,1,0:T(2,128)(2,1)S(1)}, u32[]{:S(2)}, u32[]{:S(2)}) collective-permute-start(bf16[3,1,128]{2,1,0:T(2,128)(2,1)S(1)} %get-tuple-element.27), channel_id=1, source_target_pairs={{1,0},{2,1},{3,2},{5,4},{6,5},{7,6},{9,8},{10,9},{11,10},{13,12},{... | collective-permute-start | bytes 2312 | tf_op jit(solution)/shard_map/ppermute | solution.py:19
  32.0 69.6 %collective-permute-start.14 = (bf16[3,1,128]{2,1,0:T(2,128)(2,1)S(1)}, bf16[3,1,128]{2,1,0:T(2,128)(2,1)S(1)}, u32[]{:S(2)}, u32[]{:S(2)}) collective-permute-start(bf16[3,1,128]{2,1,0:T(2,128)(2,1)S(1)} %get-tuple-element.26), channel_id=1, source_target_pairs={{0,1},{1,2},{2,3},{4,5},{5,6},{6,7},{8,9},{9,10},{10,11},{12,13},{... | collective-permute-start | bytes 2312 | tf_op jit(solution)/shard_map/ppermute | solution.py:17
  36.3 6.7 %collective-permute-start.3 = (bf16[4,1,256]{2,1,0:T(2,128)(2,1)S(1)}, bf16[4,1,256]{2,1,0:T(2,128)(2,1)S(1)}, u32[]{:S(2)}, u32[]{:S(2)}) collective-permute-start(bf16[4,1,256]{2,1,0:T(2,128)(2,1)S(1)} %get-tuple-element.19), channel_id=1, source_target_pairs={{1,0},{2,1},{3,2},{5,4},{6,5},{7,6},{9,8},{10,9},{11,10},{13,12},{... | collective-permute-start | bytes 6152 | tf_op jit(solution)/shard_map/ppermute | solution.py:19
  37.6 5.4 %collective-permute-start.2 = (bf16[4,1,256]{2,1,0:T(2,128)(2,1)S(1)}, bf16[4,1,256]{2,1,0:T(2,128)(2,1)S(1)}, u32[]{:S(2)}, u32[]{:S(2)}) collective-permute-start(bf16[4,1,256]{2,1,0:T(2,128)(2,1)S(1)} %get-tuple-element.18), channel_id=1, source_target_pairs={{0,1},{1,2},{2,3},{4,5},{5,6},{6,7},{8,9},{9,10},{10,11},{12,13},{... | collective-permute-start | bytes 6152 | tf_op jit(solution)/shard_map/ppermute | solution.py:17
  44.3 7.8 %collective-permute-start.5 = (bf16[1,64,256]{2,1,0:T(8,128)(2,1)S(1)}, bf16[1,64,256]{2,1,0:T(8,128)(2,1)S(1)}, u32[]{:S(2)}, u32[]{:S(2)}) collective-permute-start(bf16[1,64,256]{2,1,0:T(8,128)(2,1)S(1)} %get-tuple-element.23), channel_id=1, source_target_pairs={{4,0},{8,4},{12,8},{16,12},{20,16},{24,20},{28,24},{5,1},{9,5},{13... | collective-permute-start | bytes 98312 | tf_op jit(solution)/shard_map/ppermute | solution.py:19
  45.6 7.0 %collective-permute-start.4 = (bf16[1,64,256]{2,1,0:T(8,128)(2,1)S(1)}, bf16[1,64,256]{2,1,0:T(8,128)(2,1)S(1)}, u32[]{:S(2)}, u32[]{:S(2)}) collective-permute-start(bf16[1,64,256]{2,1,0:T(8,128)(2,1)S(1)} %get-tuple-element.22), channel_id=1, source_target_pairs={{0,4},{4,8},{8,12},{12,16},{16,20},{20,24},{24,28},{1,5},{5,9},{9,... | collective-permute-start | bytes 98312 | tf_op jit(solution)/shard_map/ppermute | solution.py:17
  52.6 5.0 %collective-permute-start.7 = (bf16[4,1,256]{2,1,0:T(2,128)(2,1)S(1)}, bf16[4,1,256]{2,1,0:T(2,128)(2,1)S(1)}, u32[]{:S(2)}, u32[]{:S(2)}) collective-permute-start(bf16[4,1,256]{2,1,0:T(2,128)(2,1)S(1)} %get-tuple-element.17), channel_id=1, source_target_pairs={{1,0},{2,1},{3,2},{5,4},{6,5},{7,6},{9,8},{10,9},{11,10},{13,12},{... | collective-permute-start | bytes 6152 | tf_op jit(solution)/shard_map/ppermute | solution.py:19
  53.9 4.3 %collective-permute-start.6 = (bf16[4,1,256]{2,1,0:T(2,128)(2,1)S(1)}, bf16[4,1,256]{2,1,0:T(2,128)(2,1)S(1)}, u32[]{:S(2)}, u32[]{:S(2)}) collective-permute-start(bf16[4,1,256]{2,1,0:T(2,128)(2,1)S(1)} %get-tuple-element.16), channel_id=1, source_target_pairs={{0,1},{1,2},{2,3},{4,5},{5,6},{6,7},{8,9},{9,10},{10,11},{12,13},{... | collective-permute-start | bytes 6152 | tf_op jit(solution)/shard_map/ppermute | solution.py:17
  57.6 20.6 %copy-start.9 = (bf16[3,256]{1,0:T(4,128)(2,1)S(1)}, bf16[3,256]{1,0:T(4,128)(2,1)}, u32[]{:S(2)}) copy-start(bf16[3,256]{1,0:T(4,128)(2,1)} %param.20) | copy-start | bytes 4612
  58.6 6.7 %collective-permute-start.9 = (bf16[1,64,256]{2,1,0:T(8,128)(2,1)S(1)}, bf16[1,64,256]{2,1,0:T(8,128)(2,1)S(1)}, u32[]{:S(2)}, u32[]{:S(2)}) collective-permute-start(bf16[1,64,256]{2,1,0:T(8,128)(2,1)S(1)} %get-tuple-element.21), channel_id=1, source_target_pairs={{4,0},{8,4},{12,8},{16,12},{20,16},{24,20},{28,24},{5,1},{9,5},{13... | collective-permute-start | bytes 98312 | tf_op jit(solution)/shard_map/ppermute | solution.py:19
  59.9 6.8 %collective-permute-start.8 = (bf16[1,64,256]{2,1,0:T(8,128)(2,1)S(1)}, bf16[1,64,256]{2,1,0:T(8,128)(2,1)S(1)}, u32[]{:S(2)}, u32[]{:S(2)}) collective-permute-start(bf16[1,64,256]{2,1,0:T(8,128)(2,1)S(1)} %get-tuple-element.20), channel_id=1, source_target_pairs={{0,4},{4,8},{8,12},{12,16},{16,20},{20,24},{24,28},{1,5},{5,9},{9,... | collective-permute-start | bytes 98312 | tf_op jit(solution)/shard_map/ppermute | solution.py:17
  66.7 6.0 %collective-permute-start.11 = (bf16[4,1,256]{2,1,0:T(2,128)(2,1)S(1)}, bf16[4,1,256]{2,1,0:T(2,128)(2,1)S(1)}, u32[]{:S(2)}, u32[]{:S(2)}) collective-permute-start(bf16[4,1,256]{2,1,0:T(2,128)(2,1)S(1)} %get-tuple-element.15), channel_id=1, source_target_pairs={{1,0},{2,1},{3,2},{5,4},{6,5},{7,6},{9,8},{10,9},{11,10},{13,12},{... | collective-permute-start | bytes 6152 | tf_op jit(solution)/shard_map/ppermute | solution.py:19
  68.0 5.4 %collective-permute-start.10 = (bf16[4,1,256]{2,1,0:T(2,128)(2,1)S(1)}, bf16[4,1,256]{2,1,0:T(2,128)(2,1)S(1)}, u32[]{:S(2)}, u32[]{:S(2)}) collective-permute-start(bf16[4,1,256]{2,1,0:T(2,128)(2,1)S(1)} %get-tuple-element.14), channel_id=1, source_target_pairs={{0,1},{1,2},{2,3},{4,5},{5,6},{6,7},{8,9},{9,10},{10,11},{12,13},{... | collective-permute-start | bytes 6152 | tf_op jit(solution)/shard_map/ppermute | solution.py:17
  79.2 10.4 %all-to-all-start.1 = ((f32[4,3,256]{2,1,0:T(4,128)}), f32[4,3,256]{2,1,0:T(4,128)S(1)}, u32[]{:S(2)}, u32[]{:S(2)}) async-start(f32[4,3,256]{2,1,0:T(4,128)} %fusion.11), calls=%async_computation.1 | async-start | bytes 32768 | tf_op jit(solution)/shard_map/all_to_all | solution.py:96
  85.7 89.5 %all-reduce.4.cloned.1.call-start = ((), (), s32[]{:S(2)}) async-start(), calls=%async_computation.2 | async-start | bytes 196608 | tf_op jit(solution)/shard_map/psum | solution.py:101
  89.8 85.4 %copy-start.3 = (f32[3,64,128]{2,1,0:T(8,128)S(1)}, f32[3,64,128]{2,1,0:T(8,128)}, u32[]{:S(2)}) copy-start(f32[3,64,128]{2,1,0:T(8,128)} %param.24) | copy-start | bytes 294916
  89.8 85.4 %copy-start.5 = (f32[64,128]{1,0:T(8,128)S(1)}, f32[64,128]{1,0:T(8,128)}, u32[]{:S(2)}) copy-start(f32[64,128]{1,0:T(8,128)} %param.25) | copy-start | bytes 98308
  176.2 106.5 %copy-start.4 = (f32[3,64,128]{2,1,0:T(8,128)}, f32[3,64,128]{2,1,0:T(8,128)S(1)}, u32[]{:S(2)}) copy-start(f32[3,64,128]{2,1,0:T(8,128)S(1)} %fusion.33) | copy-start | bytes 294916
Sparse Core Ops, SparseCore 0:
  101.6 73.4 all-reduce.3
where the time goes:
time: 300 us; the launch traced here: 299 us
  blocking collectives  104 us (35%)
  waiting for transfers between devices  80.6 us (27%)
  starting transfers between devices  55.9 us (19%)
  local copies, waits for them, and re-layouts  20.3 us (7%)
  other arithmetic  16.7 us (6%)
  between operations  14.5 us (5%)
  matrix products  7.25 us (2%)
    all_gather x1, blocking collectives, shards(): whole = lax.all_gather(flat_net, 'patch', axis=1, tiled=True)  104 us
    psum x1, waiting for transfers between devices, shards(): loads = lax.psum(local, 'slab')  73.6 us
    ppermute x8, starting transfers between devices, with_halo(): lax.ppermute(tail, axis, [(i, (i + 1) % count) for i in range(ends)])  35.8 us
    ppermute x8, starting transfers between devices, with_halo(): lax.ppermute(head, axis, [((i + 1) % count, i) for i in range(ends)])  10.3 us
    gather x1, local copies, waits for them, and re-layouts, shards(): picked = whole[:, (owner_ids * cells + points).reshape(-1)]  8.57 us
    scatter-add x1, other arithmetic, shards(): local.at[:, got_points.reshape(-1)]  8.21 us
    all_to_all x1, starting transfers between devices, shards(): lax.all_to_all(pull, 'patch', split_axis=0, concat_axis=0, tiled=True)  6.5 us
  transfers between devices with their start and end apart: 19, of which 6 were waited for; matrix products, arithmetic and copies ran while one was open for 10% of the time, Pallas kernels for 0%

commit v1 on v0

--- a/solution.py
+++ b/solution.py
@@ -104,7 +104,7 @@
     stiff_term = stiffness[None] * (laplace_net(bend) + 4.0 * bend)
     displacement_new = displacement + (loads - stiff_term) / (36.0 * stiffness[None])
     flat_net = displacement_new.reshape(3, -1)
-    whole = lax.all_gather(flat_net, "patch", axis=1, tiled=True)
+    whole = jnp.concatenate(lax.all_gather(flat_net, "patch"), axis=1)
     picked = whole[:, (owner_ids * cells + points).reshape(-1)]
     wall_motion = (picked * live.reshape(1, -1)).reshape(3, 1, 1, owners * capacity)
     return (state, displacement_new, wall_motion)

time: 300 us -> 209 us (0.70)
  blocking collectives: 104 us -> 7.15 us
  waiting for transfers between devices: 80.6 us -> 88.4 us
  starting transfers between devices: 55.9 us -> 48.4 us
  local copies, waits for them, and re-layouts: 20.3 us -> 26.1 us
    all_gather x1, blocking collectives: 104 us -> 7.15 us  [shards(): whole = jnp.concatenate(lax.all_gather(flat_net, 'patch'), axis=1)]
    ppermute x8, waiting for transfers between devices: 0.02 us -> 14.8 us  [with_halo(): lax.ppermute(head, axis, [((i + 1) % count, i) for i in range(ends)])]
    reshape x0 -> x1, local copies, waits for them, and re-layouts: none -> 8.38 us  [shards(): whole = jnp.concatenate(lax.all_gather(flat_net, 'patch'), axis=1)]
    ppermute x8, starting transfers between devices: 35.8 us -> 30.1 us  [with_halo(): lax.ppermute(tail, axis, [(i, (i + 1) % count) for i in range(ends)])]
    psum x1, waiting for transfers between devices: 73.6 us -> 69.6 us  [shards(): loads = lax.psum(local, 'slab')]
    ppermute x8, waiting for transfers between devices: 3.13 us -> 0.12 us  [with_halo(): lax.ppermute(tail, axis, [(i, (i + 1) % count) for i in range(ends)])]
  transfers between devices with their start and end apart: 19 -> 19, of which waited for: 6 -> 8; matrix products, arithmetic and copies ran while one was open for 10% -> 15% of each run, Pallas kernels for 0% -> 0%
where the time goes in v1:
time: 209 us; the launch traced here: 208 us
  waiting for transfers between devices  88.4 us (42%)
  starting transfers between devices  48.4 us (23%)
  local copies, waits for them, and re-layouts  26.1 us (12%)
  other arithmetic  16.6 us (8%)
  between operations  14.5 us (7%)
  matrix products  7.24 us (3%)
  blocking collectives  7.15 us (3%)
    psum x1, waiting for transfers between devices, shards(): loads = lax.psum(local, 'slab')  69.6 us
    ppermute x8, starting transfers between devices, with_halo(): lax.ppermute(tail, axis, [(i, (i + 1) % count) for i in range(ends)])  30.1 us
    ppermute x8, waiting for transfers between devices, with_halo(): lax.ppermute(head, axis, [((i + 1) % count, i) for i in range(ends)])  14.8 us
    ppermute x8, starting transfers between devices, with_halo(): lax.ppermute(head, axis, [((i + 1) % count, i) for i in range(ends)])  10.3 us
    gather x1, local copies, waits for them, and re-layouts, shards(): picked = whole[:, (owner_ids * cells + points).reshape(-1)]  8.57 us
    reshape x1, local copies, waits for them, and re-layouts, shards(): whole = jnp.concatenate(lax.all_gather(flat_net, 'patch'), axis=1)  8.38 us
    scatter-add x1, other arithmetic, shards(): local.at[:, got_points.reshape(-1)]  8.21 us
    all_gather x1, blocking collectives, shards(): whole = jnp.concatenate(lax.all_gather(flat_net, 'patch'), axis=1)  7.15 us
  transfers between devices with their start and end apart: 19, of which 8 were waited for; matrix products, arithmetic and copies ran while one was open for 15% of the time, Pallas kernels for 0%

profile of v1, /device:TPU:0, one launch (start us, length us, event | category | flops | bytes accessed | tf_op | source)
XLA Modules:
  0.0 208.4 jit_solution(11466223008417445575)
XLA Ops:
  7.2 4.4 %all-to-all-start = ((s32[4,1,256]{2,1,0:T(1,128)}), s32[4,1,256]{2,1,0:T(1,128)S(1)}, u32[]{:S(2)}, u32[]{:S(2)}) async-start(s32[4,1,256]{2,1,0:T(1,128)} %bitcast.92), calls=%async_computation | async-start | bytes 8192 | tf_op jit(solution)/shard_map/all_to_all | solution.py:97
  11.6 0.9 convert_element_type.132
  12.5 2.4 %collective-permute-start.12 = (bf16[3,1,128]{2,1,0:T(2,128)(2,1)S(1)}, bf16[3,1,128]{2,1,0:T(2,128)(2,1)S(1)}, u32[]{:S(2)}, u32[]{:S(2)}) collective-permute-start(bf16[3,1,128]{2,1,0:T(2,128)(2,1)S(1)} %get-tuple-element.28), channel_id=1, source_target_pairs={{0,1},{1,2},{2,3},{4,5},{5,6},{6,7},{8,9},{9,10},{10,11},{12,13},{... | collective-permute-start | bytes 2312 | tf_op jit(solution)/shard_map/ppermute | solution.py:17
  14.9 1.3 collective-permute-start.13
  16.2 0.9 convert_element_type.106
  17.2 3.9 %collective-permute-start = (bf16[1,64,256]{2,1,0:T(8,128)(2,1)S(1)}, bf16[1,64,256]{2,1,0:T(8,128)(2,1)S(1)}, u32[]{:S(2)}, u32[]{:S(2)}) collective-permute-start(bf16[1,64,256]{2,1,0:T(8,128)(2,1)S(1)} %get-tuple-element.24), channel_id=1, source_target_pairs={{0,4},{4,8},{8,12},{12,16},{16,20},{20,24},{24,28},{1,5},{5,9},{9,... | collective-permute-start | bytes 98312 | tf_op jit(solution)/shard_map/ppermute | solution.py:17
  21.1 1.3 collective-permute-start.1
  22.5 0.7 compare_select_fusion
  23.2 0.7 compare_select_fusion.1
  23.9 0.5 broadcast.126
  24.4 1.3 reduce.3
  25.7 0.8 broadcast_multiply_fusion
  26.5 0.7 fusion.59
  27.2 1.1 convolution_multiply_fusion.2
  28.4 1.0 fusion.70
  29.4 3.9 %collective-permute-start.14 = (bf16[3,1,128]{2,1,0:T(2,128)(2,1)S(1)}, bf16[3,1,128]{2,1,0:T(2,128)(2,1)S(1)}, u32[]{:S(2)}, u32[]{:S(2)}) collective-permute-start(bf16[3,1,128]{2,1,0:T(2,128)(2,1)S(1)} %get-tuple-element.26), channel_id=1, source_target_pairs={{0,1},{1,2},{2,3},{4,5},{5,6},{6,7},{8,9},{9,10},{10,11},{12,13},{... | collective-permute-start | bytes 2312 | tf_op jit(solution)/shard_map/ppermute | solution.py:17
  33.3 1.3 collective-permute-start.15
  34.6 4.6 %collective-permute-start.2 = (bf16[4,1,256]{2,1,0:T(2,128)(2,1)S(1)}, bf16[4,1,256]{2,1,0:T(2,128)(2,1)S(1)}, u32[]{:S(2)}, u32[]{:S(2)}) collective-permute-start(bf16[4,1,256]{2,1,0:T(2,128)(2,1)S(1)} %get-tuple-element.18), channel_id=1, source_target_pairs={{0,1},{1,2},{2,3},{4,5},{5,6},{6,7},{8,9},{9,10},{10,11},{12,13},{... | collective-permute-start | bytes 6152 | tf_op jit(solution)/shard_map/ppermute | solution.py:17
  39.2 1.3 collective-permute-start.3
  40.5 1.1 convolution_subtract_fusion.5
  41.6 1.9 collective-permute-done.3
  43.5 1.3 fusion.77
  44.9 4.5 %collective-permute-start.4 = (bf16[1,64,256]{2,1,0:T(8,128)(2,1)S(1)}, bf16[1,64,256]{2,1,0:T(8,128)(2,1)S(1)}, u32[]{:S(2)}, u32[]{:S(2)}) collective-permute-start(bf16[1,64,256]{2,1,0:T(8,128)(2,1)S(1)} %get-tuple-element.22), channel_id=1, source_target_pairs={{0,4},{4,8},{8,12},{12,16},{16,20},{20,24},{24,28},{1,5},{5,9},{9,... | collective-permute-start | bytes 98312 | tf_op jit(solution)/shard_map/ppermute | solution.py:17
  49.4 1.3 collective-permute-start.5
  50.7 1.1 convolution_multiply_fusion.1
  51.8 3.8 %collective-permute-done.5 = bf16[1,64,256]{2,1,0:T(8,128)(2,1)S(1)} collective-permute-done((bf16[1,64,256]{2,1,0:T(8,128)(2,1)S(1)}, bf16[1,64,256]{2,1,0:T(8,128)(2,1)S(1)}, u32[]{:S(2)}, u32[]{:S(2)}) %collective-permute-start.5) | collective-permute-done | bytes 32800 | tf_op jit(solution)/shard_map/ppermute | solution.py:19
  55.6 3.1 %collective-permute-start.6 = (bf16[4,1,256]{2,1,0:T(2,128)(2,1)S(1)}, bf16[4,1,256]{2,1,0:T(2,128)(2,1)S(1)}, u32[]{:S(2)}, u32[]{:S(2)}) collective-permute-start(bf16[4,1,256]{2,1,0:T(2,128)(2,1)S(1)} %get-tuple-element.16), channel_id=1, source_target_pairs={{0,1},{1,2},{2,3},{4,5},{5,6},{6,7},{8,9},{9,10},{10,11},{12,13},{... | collective-permute-start | bytes 6152 | tf_op jit(solution)/shard_map/ppermute | solution.py:17
  58.8 1.3 collective-permute-start.7
  60.3 2.3 %collective-permute-done.7 = bf16[4,1,256]{2,1,0:T(2,128)(2,1)S(1)} collective-permute-done((bf16[4,1,256]{2,1,0:T(2,128)(2,1)S(1)}, bf16[4,1,256]{2,1,0:T(2,128)(2,1)S(1)}, u32[]{:S(2)}, u32[]{:S(2)}) %collective-permute-start.7) | collective-permute-done | bytes 2080 | tf_op jit(solution)/shard_map/ppermute | solution.py:19
  62.9 4.8 %collective-permute-start.8 = (bf16[1,64,256]{2,1,0:T(8,128)(2,1)S(1)}, bf16[1,64,256]{2,1,0:T(8,128)(2,1)S(1)}, u32[]{:S(2)}, u32[]{:S(2)}) collective-permute-start(bf16[1,64,256]{2,1,0:T(8,128)(2,1)S(1)} %get-tuple-element.20), channel_id=1, source_target_pairs={{0,4},{4,8},{8,12},{12,16},{16,20},{20,24},{24,28},{1,5},{5,9},{9,... | collective-permute-start | bytes 98312 | tf_op jit(solution)/shard_map/ppermute | solution.py:17
  67.7 1.3 collective-permute-start.9
  69.3 4.2 %collective-permute-done.9 = bf16[1,64,256]{2,1,0:T(8,128)(2,1)S(1)} collective-permute-done((bf16[1,64,256]{2,1,0:T(8,128)(2,1)S(1)}, bf16[1,64,256]{2,1,0:T(8,128)(2,1)S(1)}, u32[]{:S(2)}, u32[]{:S(2)}) %collective-permute-start.9) | collective-permute-done | bytes 32800 | tf_op jit(solution)/shard_map/ppermute | solution.py:19
  73.5 2.8 %collective-permute-start.10 = (bf16[4,1,256]{2,1,0:T(2,128)(2,1)S(1)}, bf16[4,1,256]{2,1,0:T(2,128)(2,1)S(1)}, u32[]{:S(2)}, u32[]{:S(2)}) collective-permute-start(bf16[4,1,256]{2,1,0:T(2,128)(2,1)S(1)} %get-tuple-element.14), channel_id=1, source_target_pairs={{0,1},{1,2},{2,3},{4,5},{5,6},{6,7},{8,9},{9,10},{10,11},{12,13},{... | collective-permute-start | bytes 6152 | tf_op jit(solution)/shard_map/ppermute | solution.py:17
  76.4 1.3 collective-permute-start.11
  77.8 2.6 %collective-permute-done.11 = bf16[4,1,256]{2,1,0:T(2,128)(2,1)S(1)} collective-permute-done((bf16[4,1,256]{2,1,0:T(2,128)(2,1)S(1)}, bf16[4,1,256]{2,1,0:T(2,128)(2,1)S(1)}, u32[]{:S(2)}, u32[]{:S(2)}) %collective-permute-start.11) | collective-permute-done | bytes 2080 | tf_op jit(solution)/shard_map/ppermute | solution.py:19
  80.4 1.0 fusion.83
  81.4 3.9 %gather_fusion = bf16[1024,256]{1,0:T(8,128)(2,1)S(1)} fusion(bf16[128,256]{1,0:T(8,128)(2,1)S(1)} %bitcast.85, s32[1024]{0:T(1024)S(1)} %broadcast_clamp_fusion.1), kind=kCustom, calls=%fused_computation | custom fusion | bytes 1052672 | tf_op jit(solution)/shard_map/jit(_take)/gather | solution.py:84
  85.3 0.9 fusion.11
  86.3 3.6 %all-to-all-start.1 = ((f32[4,3,256]{2,1,0:T(4,128)}), f32[4,3,256]{2,1,0:T(4,128)S(1)}, u32[]{:S(2)}, u32[]{:S(2)}) async-start(f32[4,3,256]{2,1,0:T(4,128)} %fusion.11), calls=%async_computation.1 | async-start | bytes 32768 | tf_op jit(solution)/shard_map/all_to_all | solution.py:96
  89.9 3.8 %all-to-all-done.1 = f32[4,3,256]{2,1,0:T(4,128)S(1)} async-done(((f32[4,3,256]{2,1,0:T(4,128)}), f32[4,3,256]{2,1,0:T(4,128)S(1)}, u32[]{:S(2)}, u32[]{:S(2)}) %all-to-all-start.1) | async-done | bytes 12320 | tf_op jit(solution)/shard_map/all_to_all | solution.py:96
  94.0 8.2 %scatter_custom_fusion = f32[3,8192]{0,1:T(8,128)} fusion(s32[1024]{0:T(1024)S(1)} %bitcast.97, f32[1024,3]{1,0:T(8,128)S(1)} %copy.23, f32[]{:T(128)} %constant.9.clone.1), kind=kCustom, calls=%fused_computation.3 | custom fusion | flops 3072 | bytes 98308 | tf_op jit(solution)/shard_map/scatter-add | solution.py:100
  102.2 3.5 %copy.24 = f32[3,64,128]{2,1,0:T(8,128)} copy(f32[3,64,128]{0,2,1:T(8,128)} %bitcast.87) | data formatting | bytes 196608 | tf_op jit(solution)/shard_map/reshape | solution.py:102
  105.7 69.6 %all-reduce.4.cloned.1.call-done = f32[3,64,128]{2,1,0:T(8,128)} async-done(((f32[3,64,128]{2,1,0:T(8,128)}), f32[3,64,128]{2,1,0:T(8,128)}) %all-reduce.4.cloned.1.call-update) | async-done | bytes 98320 | tf_op jit(solution)/shard_map/psum | solution.py:101
  175.4 1.0 fusion.33
  176.5 7.1 %all_gather.3 = f32[4,3,8192]{2,1,0:T(4,128)S(1)} all-gather(f32[1,3,8192]{2,1,0:T(4,128)S(1)} %all_gather_reshape.3), channel_id=1, replica_groups=mesh['slab'=8,'patch'=4] {'patch'}, dimensions={0}, use_global_device_ids=true | all-gather | bytes 491520 | tf_op jit(solution)/shard_map/all_gather | solution.py:107
  183.6 8.4 %copy.25 = f32[3,4,8192]{0,2,1:T(8,128)} copy(f32[3,4,8192]{2,0,1:T(4,128)S(1)} %bitcast.88) | data formatting | bytes 786432 | tf_op jit(solution)/shard_map/reshape | solution.py:107
  192.0 8.6 %gather_fusion.1 = f32[1024,3]{1,0:T(8,128)S(1)} fusion(f32[3,32768]{0,1:T(8,128)} %bitcast.86, s32[1024]{0:T(1024)S(1)} %broadcast_clamp_fusion), kind=kCustom, calls=%fused_computation.1 | custom fusion | bytes 28672 | tf_op jit(solution)/shard_map/gather | solution.py:108
  200.8 0.8 copy.26
  (59 shorter events, 1.7 us)
Async XLA Ops:
  7.2 36.3 %copy-start = (bf16[256,256]{1,0:T(8,128)(2,1)S(1)}, bf16[256,256]{1,0:T(8,128)(2,1)}, u32[]{:S(2)}) copy-start(bf16[256,256]{1,0:T(8,128)(2,1)} %param.19) | copy-start | bytes 393220
  7.2 55.4 %copy-start.6 = (f32[2,64]{1,0:T(2,128)S(1)}, f32[2,64]{1,0:T(2,128)}, u32[]{:S(2)}) copy-start(f32[2,64]{1,0:T(2,128)} %param.15) | copy-start | bytes 1540
  7.2 61.8 %copy-start.1 = (bf16[256,256]{1,0:T(8,128)(2,1)S(1)}, bf16[256,256]{1,0:T(8,128)(2,1)}, u32[]{:S(2)}) copy-start(bf16[256,256]{1,0:T(8,128)(2,1)} %param.16) | copy-start | bytes 393220
  7.2 52.9 %copy-start.2 = (bf16[256,256]{1,0:T(8,128)(2,1)S(1)}, bf16[256,256]{1,0:T(8,128)(2,1)}, u32[]{:S(2)}) copy-start(bf16[256,256]{1,0:T(8,128)(2,1)} %param.17) | copy-start | bytes 393220
  7.2 55.3 %copy-start.8 = (bf16[256,256]{1,0:T(8,128)(2,1)S(1)}, bf16[256,256]{1,0:T(8,128)(2,1)}, u32[]{:S(2)}) copy-start(bf16[256,256]{1,0:T(8,128)(2,1)} %param.18) | copy-start | bytes 393220
  7.2 55.3 %copy-start.7 = (f32[2,64,256]{2,1,0:T(8,128)S(1)}, f32[2,64,256]{2,1,0:T(8,128)}, u32[]{:S(2)}) copy-start(f32[2,64,256]{2,1,0:T(8,128)} %param.14) | copy-start | bytes 393220
  7.2 79.0 %all-to-all-start = ((s32[4,1,256]{2,1,0:T(1,128)}), s32[4,1,256]{2,1,0:T(1,128)S(1)}, u32[]{:S(2)}, u32[]{:S(2)}) async-start(s32[4,1,256]{2,1,0:T(1,128)} %bitcast.92), calls=%async_computation | async-start | bytes 8192 | tf_op jit(solution)/shard_map/all_to_all | solution.py:97
  12.5 15.8 %collective-permute-start.12 = (bf16[3,1,128]{2,1,0:T(2,128)(2,1)S(1)}, bf16[3,1,128]{2,1,0:T(2,128)(2,1)S(1)}, u32[]{:S(2)}, u32[]{:S(2)}) collective-permute-start(bf16[3,1,128]{2,1,0:T(2,128)(2,1)S(1)} %get-tuple-element.28), channel_id=1, source_target_pairs={{0,1},{1,2},{2,3},{4,5},{5,6},{6,7},{8,9},{9,10},{10,11},{12,13},{... | collective-permute-start | bytes 2312 | tf_op jit(solution)/shard_map/ppermute | solution.py:17
  14.9 13.4 %collective-permute-start.13 = (bf16[3,1,128]{2,1,0:T(2,128)(2,1)S(1)}, bf16[3,1,128]{2,1,0:T(2,128)(2,1)S(1)}, u32[]{:S(2)}, u32[]{:S(2)}) collective-permute-start(bf16[3,1,128]{2,1,0:T(2,128)(2,1)S(1)} %get-tuple-element.29), channel_id=1, source_target_pairs={{1,0},{2,1},{3,2},{5,4},{6,5},{7,6},{9,8},{10,9},{11,10},{13,12},{... | collective-permute-start | bytes 2312 | tf_op jit(solution)/shard_map/ppermute | solution.py:19
  17.2 17.4 %collective-permute-start = (bf16[1,64,256]{2,1,0:T(8,128)(2,1)S(1)}, bf16[1,64,256]{2,1,0:T(8,128)(2,1)S(1)}, u32[]{:S(2)}, u32[]{:S(2)}) collective-permute-start(bf16[1,64,256]{2,1,0:T(8,128)(2,1)S(1)} %get-tuple-element.24), channel_id=1, source_target_pairs={{0,4},{4,8},{8,12},{12,16},{16,20},{20,24},{24,28},{1,5},{5,9},{9,... | collective-permute-start | bytes 98312 | tf_op jit(solution)/shard_map/ppermute | solution.py:17
  21.1 13.5 %collective-permute-start.1 = (bf16[1,64,256]{2,1,0:T(8,128)(2,1)S(1)}, bf16[1,64,256]{2,1,0:T(8,128)(2,1)S(1)}, u32[]{:S(2)}, u32[]{:S(2)}) collective-permute-start(bf16[1,64,256]{2,1,0:T(8,128)(2,1)S(1)} %get-tuple-element.25), channel_id=1, source_target_pairs={{4,0},{8,4},{12,8},{16,12},{20,16},{24,20},{28,24},{5,1},{9,5},{13... | collective-permute-start | bytes 98312 | tf_op jit(solution)/shard_map/ppermute | solution.py:19
  29.4 76.3 %collective-permute-start.14 = (bf16[3,1,128]{2,1,0:T(2,128)(2,1)S(1)}, bf16[3,1,128]{2,1,0:T(2,128)(2,1)S(1)}, u32[]{:S(2)}, u32[]{:S(2)}) collective-permute-start(bf16[3,1,128]{2,1,0:T(2,128)(2,1)S(1)} %get-tuple-element.26), channel_id=1, source_target_pairs={{0,1},{1,2},{2,3},{4,5},{5,6},{6,7},{8,9},{9,10},{10,11},{12,13},{... | collective-permute-start | bytes 2312 | tf_op jit(solution)/shard_map/ppermute | solution.py:17
  33.3 72.4 %collective-permute-start.15 = (bf16[3,1,128]{2,1,0:T(2,128)(2,1)S(1)}, bf16[3,1,128]{2,1,0:T(2,128)(2,1)S(1)}, u32[]{:S(2)}, u32[]{:S(2)}) collective-permute-start(bf16[3,1,128]{2,1,0:T(2,128)(2,1)S(1)} %get-tuple-element.27), channel_id=1, source_target_pairs={{1,0},{2,1},{3,2},{5,4},{6,5},{7,6},{9,8},{10,9},{11,10},{13,12},{... | collective-permute-start | bytes 2312 | tf_op jit(solution)/shard_map/ppermute | solution.py:19
  34.6 6.9 %collective-permute-start.2 = (bf16[4,1,256]{2,1,0:T(2,128)(2,1)S(1)}, bf16[4,1,256]{2,1,0:T(2,128)(2,1)S(1)}, u32[]{:S(2)}, u32[]{:S(2)}) collective-permute-start(bf16[4,1,256]{2,1,0:T(2,128)(2,1)S(1)} %get-tuple-element.18), channel_id=1, source_target_pairs={{0,1},{1,2},{2,3},{4,5},{5,6},{6,7},{8,9},{9,10},{10,11},{12,13},{... | collective-permute-start | bytes 6152 | tf_op jit(solution)/shard_map/ppermute | solution.py:17
  39.2 4.3 %collective-permute-start.3 = (bf16[4,1,256]{2,1,0:T(2,128)(2,1)S(1)}, bf16[4,1,256]{2,1,0:T(2,128)(2,1)S(1)}, u32[]{:S(2)}, u32[]{:S(2)}) collective-permute-start(bf16[4,1,256]{2,1,0:T(2,128)(2,1)S(1)} %get-tuple-element.19), channel_id=1, source_target_pairs={{1,0},{2,1},{3,2},{5,4},{6,5},{7,6},{9,8},{10,9},{11,10},{13,12},{... | collective-permute-start | bytes 6152 | tf_op jit(solution)/shard_map/ppermute | solution.py:19
  44.9 6.9 %collective-permute-start.4 = (bf16[1,64,256]{2,1,0:T(8,128)(2,1)S(1)}, bf16[1,64,256]{2,1,0:T(8,128)(2,1)S(1)}, u32[]{:S(2)}, u32[]{:S(2)}) collective-permute-start(bf16[1,64,256]{2,1,0:T(8,128)(2,1)S(1)} %get-tuple-element.22), channel_id=1, source_target_pairs={{0,4},{4,8},{8,12},{12,16},{16,20},{20,24},{24,28},{1,5},{5,9},{9,... | collective-permute-start | bytes 98312 | tf_op jit(solution)/shard_map/ppermute | solution.py:17
  49.4 6.2 %collective-permute-start.5 = (bf16[1,64,256]{2,1,0:T(8,128)(2,1)S(1)}, bf16[1,64,256]{2,1,0:T(8,128)(2,1)S(1)}, u32[]{:S(2)}, u32[]{:S(2)}) collective-permute-start(bf16[1,64,256]{2,1,0:T(8,128)(2,1)S(1)} %get-tuple-element.23), channel_id=1, source_target_pairs={{4,0},{8,4},{12,8},{16,12},{20,16},{24,20},{28,24},{5,1},{9,5},{13... | collective-permute-start | bytes 98312 | tf_op jit(solution)/shard_map/ppermute | solution.py:19
  55.6 4.6 %collective-permute-start.6 = (bf16[4,1,256]{2,1,0:T(2,128)(2,1)S(1)}, bf16[4,1,256]{2,1,0:T(2,128)(2,1)S(1)}, u32[]{:S(2)}, u32[]{:S(2)}) collective-permute-start(bf16[4,1,256]{2,1,0:T(2,128)(2,1)S(1)} %get-tuple-element.16), channel_id=1, source_target_pairs={{0,1},{1,2},{2,3},{4,5},{5,6},{6,7},{8,9},{9,10},{10,11},{12,13},{... | collective-permute-start | bytes 6152 | tf_op jit(solution)/shard_map/ppermute | solution.py:17
  58.8 3.8 %collective-permute-start.7 = (bf16[4,1,256]{2,1,0:T(2,128)(2,1)S(1)}, bf16[4,1,256]{2,1,0:T(2,128)(2,1)S(1)}, u32[]{:S(2)}, u32[]{:S(2)}) collective-permute-start(bf16[4,1,256]{2,1,0:T(2,128)(2,1)S(1)} %get-tuple-element.17), channel_id=1, source_target_pairs={{1,0},{2,1},{3,2},{5,4},{6,5},{7,6},{9,8},{10,9},{11,10},{13,12},{... | collective-permute-start | bytes 6152 | tf_op jit(solution)/shard_map/ppermute | solution.py:19
  60.2 25.1 %copy-start.9 = (bf16[3,256]{1,0:T(4,128)(2,1)S(1)}, bf16[3,256]{1,0:T(4,128)(2,1)}, u32[]{:S(2)}) copy-start(bf16[3,256]{1,0:T(4,128)(2,1)} %param.20) | copy-start | bytes 4612
  62.9 6.4 %collective-permute-start.8 = (bf16[1,64,256]{2,1,0:T(8,128)(2,1)S(1)}, bf16[1,64,256]{2,1,0:T(8,128)(2,1)S(1)}, u32[]{:S(2)}, u32[]{:S(2)}) collective-permute-start(bf16[1,64,256]{2,1,0:T(8,128)(2,1)S(1)} %get-tuple-element.20), channel_id=1, source_target_pairs={{0,4},{4,8},{8,12},{12,16},{16,20},{20,24},{24,28},{1,5},{5,9},{9,... | collective-permute-start | bytes 98312 | tf_op jit(solution)/shard_map/ppermute | solution.py:17
  67.7 5.8 %collective-permute-start.9 = (bf16[1,64,256]{2,1,0:T(8,128)(2,1)S(1)}, bf16[1,64,256]{2,1,0:T(8,128)(2,1)S(1)}, u32[]{:S(2)}, u32[]{:S(2)}) collective-permute-start(bf16[1,64,256]{2,1,0:T(8,128)(2,1)S(1)} %get-tuple-element.21), channel_id=1, source_target_pairs={{4,0},{8,4},{12,8},{16,12},{20,16},{24,20},{28,24},{5,1},{9,5},{13... | collective-permute-start | bytes 98312 | tf_op jit(solution)/shard_map/ppermute | solution.py:19
  73.5 4.3 %collective-permute-start.10 = (bf16[4,1,256]{2,1,0:T(2,128)(2,1)S(1)}, bf16[4,1,256]{2,1,0:T(2,128)(2,1)S(1)}, u32[]{:S(2)}, u32[]{:S(2)}) collective-permute-start(bf16[4,1,256]{2,1,0:T(2,128)(2,1)S(1)} %get-tuple-element.14), channel_id=1, source_target_pairs={{0,1},{1,2},{2,3},{4,5},{5,6},{6,7},{8,9},{9,10},{10,11},{12,13},{... | collective-permute-start | bytes 6152 | tf_op jit(solution)/shard_map/ppermute | solution.py:17
  76.4 4.0 %collective-permute-start.11 = (bf16[4,1,256]{2,1,0:T(2,128)(2,1)S(1)}, bf16[4,1,256]{2,1,0:T(2,128)(2,1)S(1)}, u32[]{:S(2)}, u32[]{:S(2)}) collective-permute-start(bf16[4,1,256]{2,1,0:T(2,128)(2,1)S(1)} %get-tuple-element.15), channel_id=1, source_target_pairs={{1,0},{2,1},{3,2},{5,4},{6,5},{7,6},{9,8},{10,9},{11,10},{13,12},{... | collective-permute-start | bytes 6152 | tf_op jit(solution)/shard_map/ppermute | solution.py:19
  86.3 7.5 %all-to-all-start.1 = ((f32[4,3,256]{2,1,0:T(4,128)}), f32[4,3,256]{2,1,0:T(4,128)S(1)}, u32[]{:S(2)}, u32[]{:S(2)}) async-start(f32[4,3,256]{2,1,0:T(4,128)} %fusion.11), calls=%async_computation.1 | async-start | bytes 32768 | tf_op jit(solution)/shard_map/all_to_all | solution.py:96
  89.9 85.5 %all-reduce.4.cloned.1.call-start = ((), (), s32[]{:S(2)}) async-start(), calls=%async_computation.2 | async-start | bytes 196608 | tf_op jit(solution)/shard_map/psum | solution.py:101
  94.0 81.4 %copy-start.3 = (f32[3,64,128]{2,1,0:T(8,128)S(1)}, f32[3,64,128]{2,1,0:T(8,128)}, u32[]{:S(2)}) copy-start(f32[3,64,128]{2,1,0:T(8,128)} %param.24) | copy-start | bytes 294916
  94.0 81.4 %copy-start.5 = (f32[64,128]{1,0:T(8,128)S(1)}, f32[64,128]{1,0:T(8,128)}, u32[]{:S(2)}) copy-start(f32[64,128]{1,0:T(8,128)} %param.25) | copy-start | bytes 98308
  176.4 15.6 %copy-start.4 = (f32[3,64,128]{2,1,0:T(8,128)}, f32[3,64,128]{2,1,0:T(8,128)S(1)}, u32[]{:S(2)}) copy-start(f32[3,64,128]{2,1,0:T(8,128)S(1)} %fusion.33) | copy-start | bytes 294916
Sparse Core Ops, SparseCore 0:
  105.8 69.5 all-reduce.3
